TPU v7x, 32 devices: a whole 2x2x4 slice. The times are simulated.
32 devices in a mesh: elem: 8 (over z, x), span: 4 (over y, core).
Axes of the slice: x: 2, y: 2, z: 4, core: 2. Of those that a mesh axis runs over, the one named last changes fastest.
Arguments:
- column_state: bfloat16 [24576, 1152], P(('elem', 'span')), may hold values from -6 to 6
- counts: int32 [32], replicated, may hold values from 128 to 768, as said below
- edge_index: int32 [32, 4, 16], P(('elem', 'span')), may hold values from 0 to 127, as said below
- encode_first: bfloat16 [3, 32, 16], replicated, may hold values from -0.875 to 0.875
- encode_second: bfloat16 [8, 3, 32, 32], replicated, may hold values from -0.625 to 0.625
- middle_first: bfloat16 [3, 64, 32], replicated, may hold values from -0.625 to 0.625
- middle_second: bfloat16 [8, 3, 64, 64], replicated, may hold values from -0.4375 to 0.4375
- decode_first: bfloat16 [3, 32, 96], replicated, may hold values from -0.375 to 0.375
- decode_second: bfloat16 [8, 3, 32, 32], replicated, may hold values from -0.625 to 0.625
- output_weight: bfloat16 [3, 16, 32], replicated, may hold values from -0.625 to 0.625
Outputs:
- tendencies: bfloat16 [24576, 1152], P(('elem', 'span'))
Inputs may be any that keep to these rules, and one draw needn't show every extreme that they name: counts sum to 8192. `edge_index`: the 64 entries of one owner are distinct.
All inputs are finite; a program needn't handle non-finite values.
Results may differ from a plain program's by a relative error of at most 0.0085.
Values may be sent and summed in bfloat16 or wider, within the bound.
A program may use at most 64 MiB of HBM per device.

v0:
```python
import math
import jax
import jax.numpy as jnp
from jax import lax
from jax.sharding import PartitionSpec as P

LEV = 72
F_IN = 16
F_OUT = 16
DEPTH = 8
SPAN = 256


def extended(cells, sides, width):
    for axis, dim in sides:
        count = lax.axis_size(axis)
        head = lax.slice_in_dim(cells, 0, width, axis=dim)
        tail = lax.slice_in_dim(cells, cells.shape[dim] - width, cells.shape[dim], axis=dim)
        cells = jnp.concatenate(
            [
                lax.ppermute(tail, axis, [(i, (i + 1) % count) for i in range(count)]),
                cells,
                lax.ppermute(head, axis, [((i + 1) % count, i) for i in range(count)]),
            ],
            axis=dim,
        )
    return cells


def conv_levels(profile, weight):
    levels = profile.shape[1]
    padded = jnp.pad(profile, ((0, 0), (1, 1), (0, 0)))
    stacked = jnp.concatenate(
        [padded[:, tap_index : tap_index + levels, :] for tap_index in range(3)], axis=0
    )
    flat_weight = weight.transpose(1, 0, 2).reshape(weight.shape[1], 3 * weight.shape[2])
    return jnp.einsum("ok,kln->oln", flat_weight, stacked, preferred_element_type=jnp.float32)


def residual_stack(hidden, stacked_weights):
    for layer_index in range(DEPTH):
        update = jax.nn.silu(conv_levels(hidden, stacked_weights[layer_index]))
        hidden = (hidden.astype(jnp.float32) + update).astype(jnp.bfloat16)
    return hidden


def network(columns, weights):
    (
        encode_first,
        encode_second,
        middle_first,
        middle_second,
        decode_first,
        decode_second,
        output_weight,
    ) = weights
    inputs = columns.reshape(columns.shape[0], F_IN, LEV).transpose(1, 2, 0)
    hidden = jax.nn.silu(conv_levels(inputs, encode_first)).astype(jnp.bfloat16)
    skipped = residual_stack(hidden, encode_second)
    pooled = (
        0.5 * (skipped[:, 0::2].astype(jnp.float32) + skipped[:, 1::2].astype(jnp.float32))
    ).astype(jnp.bfloat16)
    middle = jax.nn.silu(conv_levels(pooled, middle_first)).astype(jnp.bfloat16)
    middle = residual_stack(middle, middle_second)
    raised = jnp.repeat(middle, 2, axis=1)
    joined = jnp.concatenate([raised, skipped], axis=0)
    decoded = jax.nn.silu(conv_levels(joined, decode_first)).astype(jnp.bfloat16)
    decoded = residual_stack(decoded, decode_second)
    result = conv_levels(decoded, output_weight).astype(jnp.bfloat16)
    return result.transpose(2, 0, 1).reshape(columns.shape[0], F_OUT * LEV)


def on_device(
    column_state,
    counts,
    edge_index,
    encode_first,
    encode_second,
    middle_first,
    middle_second,
    decode_first,
    decode_second,
    output_weight,
):
    weights = (
        encode_first,
        encode_second,
        middle_first,
        middle_second,
        decode_first,
        decode_second,
        output_weight,
    )
    devices = lax.axis_size(("elem", "span"))
    device_index = lax.axis_index(("elem", "span"))
    col_max = column_state.shape[0]
    feat_in = column_state.shape[1]
    feat_out = F_OUT * LEV
    slot_count = col_max // devices
    offsets = jnp.concatenate([jnp.zeros((1,), jnp.int32), jnp.cumsum(counts)])
    rank_start = offsets[device_index]
    slot_grid = column_state.reshape(slot_count, devices, feat_in)
    outgoing = jnp.roll(slot_grid, rank_start, axis=1)
    arrived = lax.all_to_all(outgoing, ("elem", "span"), split_axis=1, concat_axis=1, tiled=True)
    block_ranks = jnp.arange(SPAN, dtype=jnp.int32) * devices + device_index
    source = jnp.sum((offsets[None, 1:] <= block_ranks[:, None]).astype(jnp.int32), axis=1)
    within = block_ranks - offsets[source]
    flat_index = within // devices * devices + source
    dense_rows = arrived.reshape(slot_count * devices, feat_in)[flat_index]
    block_rows = math.gcd(SPAN, 128)
    computed = lax.map(
        lambda rows_block: network(rows_block, weights), dense_rows.reshape(-1, block_rows, feat_in)
    )
    computed = computed.reshape(SPAN, feat_out)
    slot_back = (
        jnp.zeros((slot_count * devices, feat_out), jnp.bfloat16).at[flat_index].set(computed)
    )
    slot_back = slot_back.reshape(slot_count, devices, feat_out)
    returned = lax.all_to_all(slot_back, ("elem", "span"), split_axis=1, concat_axis=1, tiled=True)
    owned = jnp.roll(returned, -rank_start, axis=1).reshape(col_max, feat_out)
    edge_local = edge_index[0]
    edge_rows = owned[edge_local]
    across = extended(edge_rows[0:2], (("elem", 0),), 1)
    upward = extended(edge_rows[2:4], (("span", 0),), 1)
    edge_float = edge_rows.astype(jnp.float32)
    west_edge = 0.5 * (edge_float[0] + across[0].astype(jnp.float32))
    east_edge = 0.5 * (edge_float[1] + across[3].astype(jnp.float32))
    south_edge = 0.5 * (edge_float[2] + upward[0].astype(jnp.float32))
    north_edge = 0.5 * (edge_float[3] + upward[3].astype(jnp.float32))
    merged = jnp.stack([west_edge, east_edge, south_edge, north_edge], axis=0).astype(jnp.bfloat16)
    owned = owned.at[edge_local.reshape(-1)].set(merged.reshape(-1, feat_out))
    return owned


def solution(mesh):
    return jax.shard_map(
        on_device,
        mesh=mesh,
        in_specs=(
            P(("elem", "span"), None),
            P(),
            P(("elem", "span"), None, None),
            P(),
            P(),
            P(),
            P(),
            P(),
            P(),
            P(),
        ),
        out_specs=P(("elem", "span"), None),
        check_vma=False,
    )
```

profile of v0, /device:TPU:0, one launch (start us, length us, event | category | flops | bytes accessed | tf_op | source)
XLA Modules:
  0.0 176.2 jit_solution(497506823206754736)
XLA Ops:
  0.0 0.7 copy.116
  1.0 0.6 dynamic_slice.13
  3.5 2.8 %fusion.332 = bf16[24,32,1152]{2,1,0:T(8,128)(2,1)S(1)} fusion(s32[]{:T(128)S(6)} %select_n.75, bf16[24,32,1152]{2,1,0:T(8,128)(2,1)} %bitcast.526), kind=kLoop, calls=%fused_computation.341 | loop fusion | flops 3538944 | bytes 3538948 | tf_op jit(solution)/shard_map/jit(_roll_dynamic)/concatenate | solution.py:103
  6.2 1.7 copy.117
  8.0 7.6 %all-to-all-start = ((bf16[24,32,1152]{2,0,1:T(8,128)(2,1)}), bf16[24,32,1152]{2,0,1:T(8,128)(2,1)}, u32[]{:S(2)}, u32[]{:S(2)}) async-start(bf16[24,32,1152]{2,0,1:T(8,128)(2,1)} %copy.117), calls=%async_computation | async-start | bytes 3538944 | tf_op jit(solution)/shard_map/all_to_all | solution.py:104
  16.2 0.6 fusion.351
  16.8 0.7 fusion.350
  17.6 3.6 %compare_select_fusion.3 = (s32[256,1]{0,1:T(1,128)S(1)}, s32[256,1]{0,1:T(1,128)S(1)}) fusion(s32[]{:T(128)} %bitcast.132, s32[]{:T(128)} %bitcast.133, s32[]{:T(128)} %bitcast.134, s32[]{:T(128)} %bitcast.135, s32[]{:T(128)} %bitcast.136, s32[]{:T(128)} %bitcast.137, s32[256,1]{0,1:T(1,128)S(1)} %bitcast.538), kind=kLoop, calls=%fused_computation.397 | loop fusion | flops 3840 | bytes 3096 | tf_op jit(solution)/shard_map/gather | solution.py:107
  21.3 16.4 %select_select_fusion = s32[256]{0:T(256)S(1)} fusion(pred[256]{0:T(512)(128)(4,1)S(1)} %get-tuple-element.217, pred[256]{0:T(512)(128)(4,1)S(1)} %get-tuple-element.216, pred[256]{0:T(512)(128)(4,1)S(1)} %get-tuple-element.215, pred[256]{0:T(512)(128)(4,1)S(1)} %get-tuple-element.214, pred[256]{0:T(512)(128)(4,1)S(1)} %get-tuple-element.213, ...), kind=kLoop, calls=%fused_computation.408 | loop fusion | flops 6656 | bytes 8808 | tf_op jit(solution)/shard_map/gather | solution.py:107
  37.7 19.6 %all-to-all-done = bf16[24,32,1152]{2,0,1:T(8,128)(2,1)} async-done(((bf16[24,32,1152]{2,0,1:T(8,128)(2,1)}), bf16[24,32,1152]{2,0,1:T(8,128)(2,1)}, u32[]{:S(2)}, u32[]{:S(2)}) %all-to-all-start) | async-done | bytes 1769504 | tf_op jit(solution)/shard_map/all_to_all | solution.py:104
  57.3 1.7 copy.118
  59.0 1.3 gather_fusion
  60.3 53.1 %while.12 = (s32[]{:T(128)}, bf16[2,128,1152]{2,1,0:T(8,128)(2,1)}, bf16[2,128,1152]{2,1,0:T(8,128)(2,1)S(1)}, bf16[3,32,16]{1,2,0:T(8,128)(2,1)S(1)}, bf16[8,3,...) while((s32[]{:T(128)}, bf16[2,128,1152]{2,1,0:T(8,128)(2,1)}, ...), condition=%wide.region_3.5_spmd, body=%wide.region_2.4_spmd.sunk | while | flops 2317344768 | bytes 136280240 | solution.py:111
  62.7 0.5 multiply_convert_fusion.8
  68.8 0.5 multiply_convert_fusion.10
  69.6 0.6 add_convert_fusion.56
  70.6 0.6 add_convert_fusion.57
  71.5 0.6 add_convert_fusion.58
  72.5 0.6 add_convert_fusion.59
  73.5 0.6 add_convert_fusion.60
  74.4 0.6 add_convert_fusion.61
  75.4 0.6 add_convert_fusion.62
  76.3 0.6 add_convert_fusion.63
  77.4 0.6 fusion.498
  78.0 1.6 multiply_convert_fusion.11
  86.1 0.8 copy-done.9
  95.2 0.5 multiply_convert_fusion.10
  96.1 0.6 add_convert_fusion.56
  97.0 0.6 add_convert_fusion.57
  98.0 0.6 add_convert_fusion.58
  99.0 0.6 add_convert_fusion.59
  99.9 0.6 add_convert_fusion.60
  100.9 0.6 add_convert_fusion.61
  101.8 0.6 add_convert_fusion.62
  102.8 0.6 add_convert_fusion.63
  103.9 0.6 fusion.498
  104.5 1.6 multiply_convert_fusion.11
  112.6 0.8 copy-done.9
  113.4 2.7 %scatter_custom_fusion = bf16[768,1152]{1,0:T(8,128)(2,1)S(1)} fusion(s32[256]{0:T(256)} %bitcast.541, bf16[256,1152]{1,0:T(8,128)(2,1)} %bitcast.545, bf16[]{:T(256)} %constant.112.clone.1), kind=kCustom, calls=%fused_computation.342 | custom fusion | bytes 1769984 | tf_op jit(solution)/shard_map/scatter | solution.py:116
  116.2 1.7 copy.126
  117.9 3.8 %all-to-all-start.1 = ((bf16[24,32,1152]{2,0,1:T(8,128)(2,1)}), bf16[24,32,1152]{2,0,1:T(8,128)(2,1)S(1)}, u32[]{:S(2)}, u32[]{:S(2)}) async-start(bf16[24,32,1152]{2,0,1:T(8,128)(2,1)} %copy.126), calls=%async_computation.1 | async-start | bytes 3538944 | tf_op jit(solution)/shard_map/all_to_all | solution.py:119
  122.6 40.9 %all-to-all-done.1 = bf16[24,32,1152]{2,0,1:T(8,128)(2,1)S(1)} async-done(((bf16[24,32,1152]{2,0,1:T(8,128)(2,1)}), bf16[24,32,1152]{2,0,1:T(8,128)(2,1)S(1)}, u32[]{:S(2)}, u32[]{:S(2)}) %all-to-all-start.1) | async-done | bytes 1769504 | tf_op jit(solution)/shard_map/all_to_all | solution.py:119
  163.5 0.7 fusion.331
  164.4 0.7 gather_fusion.1
  165.2 1.5 collective-permute-start
  167.2 3.3 %collective-permute-start.1 = (bf16[1,16,1152]{2,1,0:T(8,128)(2,1)S(1)}, bf16[1,16,1152]{2,1,0:T(8,128)(2,1)S(1)}, u32[]{:S(2)}, u32[]{:S(2)}) collective-permute-start(bf16[1,16,1152]{2,1,0:T(8,128)(2,1)S(1)} %get-tuple-element.335), channel_id=1, source_target_pairs={{4,0},{8,4},{12,8},{16,12},{20,16},{24,20},{28,24},{0,28},{5,1},{9... | collective-permute-start | bytes 110600 | tf_op jit(solution)/shard_map/ppermute | solution.py:23
  170.5 1.4 collective-permute-done
  172.4 3.9 %scatter_fusion = bf16[768,1152]{1,0:T(8,128)(2,1)} fusion(bf16[768,1152]{1,0:T(8,128)(2,1)} %bitcast.523, s32[64]{0:T(128)S(1)} %fusion.347, bf16[64,1152]{1,0:T(8,128)(2,1)S(1)} %bitcast.537), kind=kCustom, calls=%fused_computation.3 | custom fusion | bytes 442624 | tf_op jit(solution)/shard_map/scatter | solution.py:131
  (202 shorter events, 36.6 us)
Async XLA Ops:
  8.0 7.6 %copy-start.5 = (bf16[3,16,32]{2,1,0:T(8,128)(2,1)S(1)}, bf16[3,16,32]{2,1,0:T(8,128)(2,1)}, u32[]{:S(2)}) copy-start(bf16[3,16,32]{2,1,0:T(8,128)(2,1)} %param.23) | copy-start | bytes 9220
  8.0 7.6 %copy-start.4 = (bf16[3,32,96]{2,1,0:T(8,128)(2,1)S(1)}, bf16[3,32,96]{2,1,0:T(8,128)(2,1)}, u32[]{:S(2)}) copy-start(bf16[3,32,96]{2,1,0:T(8,128)(2,1)} %param.21) | copy-start | bytes 55300
  8.0 7.7 %copy-start.2 = (bf16[8,3,32,32]{3,2,1,0:T(8,128)(2,1)S(1)}, bf16[8,3,32,32]{3,2,1,0:T(8,128)(2,1)}, u32[]{:S(2)}) copy-start(bf16[8,3,32,32]{3,2,1,0:T(8,128)(2,1)} %param.18) | copy-start | bytes 147460
  8.0 7.8 %copy-start.3 = (bf16[8,3,32,32]{3,2,1,0:T(8,128)(2,1)S(1)}, bf16[8,3,32,32]{3,2,1,0:T(8,128)(2,1)}, u32[]{:S(2)}) copy-start(bf16[8,3,32,32]{3,2,1,0:T(8,128)(2,1)} %param.22) | copy-start | bytes 147460
  8.0 8.0 %copy-start.1 = (bf16[8,3,64,64]{3,2,1,0:T(8,128)(2,1)S(1)}, bf16[8,3,64,64]{3,2,1,0:T(8,128)(2,1)}, u32[]{:S(2)}) copy-start(bf16[8,3,64,64]{3,2,1,0:T(8,128)(2,1)} %param.20) | copy-start | bytes 589828
  8.0 49.3 %all-to-all-start = ((bf16[24,32,1152]{2,0,1:T(8,128)(2,1)}), bf16[24,32,1152]{2,0,1:T(8,128)(2,1)}, u32[]{:S(2)}, u32[]{:S(2)}) async-start(bf16[24,32,1152]{2,0,1:T(8,128)(2,1)} %copy.117), calls=%async_computation | async-start | bytes 3538944 | tf_op jit(solution)/shard_map/all_to_all | solution.py:104
  37.7 21.3 %copy-start.7 = (s32[256,1]{0,1:T(1,128)}, s32[256,1]{0,1:T(1,128)S(1)}, u32[]{:S(2)}) copy-start(s32[256,1]{0,1:T(1,128)S(1)} %compare_select_fusion) | copy-start | bytes 3076
  59.0 1.3 copy-start.10
  59.0 1.3 copy-start.11
  85.0 1.1 copy-start.8
  86.1 0.8 copy-start.9
  111.5 1.1 copy-start.8
  112.6 0.8 copy-start.9
  117.9 4.5 %copy-start.6 = (s32[1,4,16]{2,1,0:T(4,128)S(1)}, s32[1,4,16]{2,1,0:T(4,128)}, u32[]{:S(2)}) copy-start(s32[1,4,16]{2,1,0:T(4,128)} %param.16) | copy-start | bytes 772
  117.9 45.6 %all-to-all-start.1 = ((bf16[24,32,1152]{2,0,1:T(8,128)(2,1)}), bf16[24,32,1152]{2,0,1:T(8,128)(2,1)S(1)}, u32[]{:S(2)}, u32[]{:S(2)}) async-start(bf16[24,32,1152]{2,0,1:T(8,128)(2,1)} %copy.126), calls=%async_computation.1 | async-start | bytes 3538944 | tf_op jit(solution)/shard_map/all_to_all | solution.py:119
  164.4 7.9 %copy-start = (bf16[24,32,1152]{2,1,0:T(8,128)(2,1)}, bf16[24,32,1152]{2,1,0:T(8,128)(2,1)S(1)}, u32[]{:S(2)}) copy-start(bf16[24,32,1152]{2,1,0:T(8,128)(2,1)S(1)} %copy.127) | copy-start | bytes 5308420
  165.2 6.7 %collective-permute-start = (bf16[1,16,1152]{2,1,0:T(8,128)(2,1)S(1)}, bf16[1,16,1152]{2,1,0:T(8,128)(2,1)S(1)}, u32[]{:S(2)}, u32[]{:S(2)}) collective-permute-start(bf16[1,16,1152]{2,1,0:T(8,128)(2,1)S(1)} %get-tuple-element.332), channel_id=1, source_target_pairs={{0,4},{4,8},{8,12},{12,16},{16,20},{20,24},{24,28},{28,0},{1,5},{5... | collective-permute-start | bytes 110600 | tf_op jit(solution)/shard_map/ppermute | solution.py:21
  166.7 5.3 %collective-permute-start.3 = (bf16[1,16,1152]{2,1,0:T(8,128)(2,1)S(1)}, bf16[1,16,1152]{2,1,0:T(8,128)(2,1)S(1)}, u32[]{:S(2)}, u32[]{:S(2)}) collective-permute-start(bf16[1,16,1152]{2,1,0:T(8,128)(2,1)S(1)} %get-tuple-element.333), channel_id=1, source_target_pairs={{1,0},{2,1},{3,2},{0,3},{5,4},{6,5},{7,6},{4,7},{9,8},{10,9},{11,1... | collective-permute-start | bytes 110600 | tf_op jit(solution)/shard_map/ppermute | solution.py:23
  167.2 4.8 %collective-permute-start.2 = (bf16[1,16,1152]{2,1,0:T(8,128)(2,1)S(1)}, bf16[1,16,1152]{2,1,0:T(8,128)(2,1)S(1)}, u32[]{:S(2)}, u32[]{:S(2)}) collective-permute-start(bf16[1,16,1152]{2,1,0:T(8,128)(2,1)S(1)} %get-tuple-element.334), channel_id=1, source_target_pairs={{0,1},{1,2},{2,3},{3,0},{4,5},{5,6},{6,7},{7,4},{8,9},{9,10},{10,1... | collective-permute-start | bytes 110600 | tf_op jit(solution)/shard_map/ppermute | solution.py:21
  167.2 5.1 %collective-permute-start.1 = (bf16[1,16,1152]{2,1,0:T(8,128)(2,1)S(1)}, bf16[1,16,1152]{2,1,0:T(8,128)(2,1)S(1)}, u32[]{:S(2)}, u32[]{:S(2)}) collective-permute-start(bf16[1,16,1152]{2,1,0:T(8,128)(2,1)S(1)} %get-tuple-element.335), channel_id=1, source_target_pairs={{4,0},{8,4},{12,8},{16,12},{20,16},{24,20},{28,24},{0,28},{5,1},{9... | collective-permute-start | bytes 110600 | tf_op jit(solution)/shard_map/ppermute | solution.py:23
where the time goes:
time: 177 us; the launch traced here: 176 us
  waiting for transfers between devices  62.3 us (35%)
  local copies, waits for them, and re-layouts  37.2 us (21%)
  matrix products  31.5 us (18%)
  other arithmetic  24.5 us (14%)
  starting transfers between devices  16.7 us (9%)
  between operations  2.82 us (2%)
    all_to_all x1, waiting for transfers between devices, on_device(): lax.all_to_all(slot_back, ('elem', 'span'), split_axis=1, concat_axis=1,...  40.9 us
    dot_general x56, matrix products, conv_levels(): jnp.einsum('ok,kln->oln', flat_weight, stacked, preferred_element_type=jn...  31.5 us
    gather x3, other arithmetic, on_device(): within = block_ranks - offsets[source]  20.1 us
    all_to_all x1, waiting for transfers between devices, on_device(): lax.all_to_all(outgoing, ('elem', 'span'), split_axis=1, concat_axis=1, t...  19.6 us
    slice x56, local copies, waits for them, and re-layouts, conv_levels(): padded[:, tap_index:tap_index + levels, :]  12 us
    all_to_all x1, starting transfers between devices, on_device(): lax.all_to_all(outgoing, ('elem', 'span'), split_axis=1, concat_axis=1, t...  7.56 us
    scatter x1, local copies, waits for them, and re-layouts, on_device(): owned = owned.at[edge_local.reshape(-1)].set(merged.reshape(-1, feat_out))  3.86 us
    all_to_all x1, starting transfers between devices, on_device(): lax.all_to_all(slot_back, ('elem', 'span'), split_axis=1, concat_axis=1,...  3.83 us
  transfers between devices with their start and end apart: 6, of which 4 were waited for; matrix products, arithmetic and copies ran while one was open for 13% of the time, Pallas kernels for 0%

commit v1 on v0

--- a/solution.py
+++ b/solution.py
@@ -116,7 +116,15 @@
         jnp.zeros((slot_count * devices, feat_out), jnp.bfloat16).at[flat_index].set(computed)
     )
     slot_back = slot_back.reshape(slot_count, devices, feat_out)
-    returned = lax.all_to_all(slot_back, ("elem", "span"), split_axis=1, concat_axis=1, tiled=True)
+    returned = jnp.concatenate(
+        lax.all_to_all(
+            jnp.stack(jnp.split(slot_back, lax.axis_size(("elem", "span")), axis=1)),
+            ("elem", "span"),
+            0,
+            0,
+        ),
+        axis=1,
+    )
     owned = jnp.roll(returned, -rank_start, axis=1).reshape(col_max, feat_out)
     edge_local = edge_index[0]
     edge_rows = owned[edge_local]

time: 177 us -> 198 us (1.12)
  local copies, waits for them, and re-layouts: 37.2 us -> 58.5 us
    unnamed x20 -> x51, local copies, waits for them, and re-layouts: 0.05 us -> 19.6 us
    split x0 -> x2, local copies, waits for them, and re-layouts: none -> 2.88 us  [on_device(): jnp.split(slot_back, lax.axis_size(('elem', 'span')), axis=1)]
  transfers between devices with their start and end apart: 6 -> 6, of which waited for: 4 -> 4; matrix products, arithmetic and copies ran while one was open for 13% -> 11% of each run, Pallas kernels for 0% -> 0%
where the time goes in v1:
time: 198 us
  waiting for transfers between devices  62.3 us (31%)
  local copies, waits for them, and re-layouts  58.5 us (30%)
  matrix products  31.5 us (16%)
  other arithmetic  24.5 us (12%)
  starting transfers between devices  16.7 us (8%)
  between operations  2.86 us (1%)
    all_to_all x1, waiting for transfers between devices, on_device(): lax.all_to_all(jnp.stack(jnp.split(slot_back, lax.axis_size(('elem', 'spa...  40.9 us
    dot_general x56, matrix products, conv_levels(): jnp.einsum('ok,kln->oln', flat_weight, stacked, preferred_element_type=jn...  31.5 us
    gather x3, other arithmetic, on_device(): within = block_ranks - offsets[source]  20.1 us
    all_to_all x1, waiting for transfers between devices, on_device(): lax.all_to_all(outgoing, ('elem', 'span'), split_axis=1, concat_axis=1, t...  19.6 us
    unnamed x51, local copies, waits for them, and re-layouts  19.6 us
    slice x56, local copies, waits for them, and re-layouts, conv_levels(): padded[:, tap_index:tap_index + levels, :]  12 us
    all_to_all x1, starting transfers between devices, on_device(): lax.all_to_all(outgoing, ('elem', 'span'), split_axis=1, concat_axis=1, t...  7.56 us
  transfers between devices with their start and end apart: 6, of which 4 were waited for; matrix products, arithmetic and copies ran while one was open for 11% of the time, Pallas kernels for 0%

profile of v1, /device:TPU:0, one launch (start us, length us, event | category | flops | bytes accessed | tf_op | source)
XLA Modules:
  0.0 197.6 jit_solution(8230490490805300454)
XLA Ops:
  0.0 0.7 copy.1201
  3.5 2.8 %fusion.332 = bf16[24,32,1152]{2,1,0:T(8,128)(2,1)S(1)} fusion(s32[]{:T(128)S(6)} %select_n.75, bf16[24,32,1152]{2,1,0:T(8,128)(2,1)} %bitcast.595), kind=kLoop, calls=%fused_computation.341 | loop fusion | flops 3538944 | bytes 3538948 | tf_op jit(solution)/shard_map/jit(_roll_dynamic)/concatenate | solution.py:103
  6.2 1.7 copy.1202
  8.0 7.6 %all-to-all-start = ((bf16[24,32,1152]{2,0,1:T(8,128)(2,1)}), bf16[24,32,1152]{2,0,1:T(8,128)(2,1)}, u32[]{:S(2)}, u32[]{:S(2)}) async-start(bf16[24,32,1152]{2,0,1:T(8,128)(2,1)} %copy.1202), calls=%async_computation | async-start | bytes 3538944 | tf_op jit(solution)/shard_map/all_to_all | solution.py:104
  16.8 0.7 fusion.352
  17.6 3.6 %compare_select_fusion.3 = (s32[256,1]{0,1:T(1,128)S(1)}, s32[256,1]{0,1:T(1,128)S(1)}) fusion(s32[]{:T(128)} %bitcast.132, s32[]{:T(128)} %bitcast.133, s32[]{:T(128)} %bitcast.134, s32[]{:T(128)} %bitcast.135, s32[]{:T(128)} %bitcast.136, s32[]{:T(128)} %bitcast.137, s32[256,1]{0,1:T(1,128)S(1)} %bitcast.607), kind=kLoop, calls=%fused_computation.429 | loop fusion | flops 3840 | bytes 3096 | tf_op jit(solution)/shard_map/gather | solution.py:107
  21.3 16.4 %select_select_fusion = s32[256]{0:T(256)S(1)} fusion(pred[256]{0:T(512)(128)(4,1)S(1)} %get-tuple-element.497, pred[256]{0:T(512)(128)(4,1)S(1)} %get-tuple-element.496, pred[256]{0:T(512)(128)(4,1)S(1)} %get-tuple-element.495, pred[256]{0:T(512)(128)(4,1)S(1)} %get-tuple-element.494, pred[256]{0:T(512)(128)(4,1)S(1)} %get-tuple-element.493, ...), kind=kLoop, calls=%fused_computation.440 | loop fusion | flops 6656 | bytes 8808 | tf_op jit(solution)/shard_map/gather | solution.py:107
  37.7 19.6 %all-to-all-done = bf16[24,32,1152]{2,0,1:T(8,128)(2,1)} async-done(((bf16[24,32,1152]{2,0,1:T(8,128)(2,1)}), bf16[24,32,1152]{2,0,1:T(8,128)(2,1)}, u32[]{:S(2)}, u32[]{:S(2)}) %all-to-all-start) | async-done | bytes 1769504 | tf_op jit(solution)/shard_map/all_to_all | solution.py:104
  57.3 1.7 copy.1203
  59.0 1.3 gather_fusion
  60.3 53.1 %while.12 = (s32[]{:T(128)}, bf16[2,128,1152]{2,1,0:T(8,128)(2,1)}, bf16[2,128,1152]{2,1,0:T(8,128)(2,1)S(1)}, bf16[3,32,16]{1,2,0:T(8,128)(2,1)S(1)}, bf16[8,3,...) while((s32[]{:T(128)}, bf16[2,128,1152]{2,1,0:T(8,128)(2,1)}, ...), condition=%wide.region_3.5_spmd, body=%wide.region_2.4_spmd.sunk | while | flops 2317344768 | bytes 136280240 | solution.py:111
  69.6 0.6 add_convert_fusion.56
  70.6 0.6 add_convert_fusion.57
  71.5 0.6 add_convert_fusion.58
  72.5 0.6 add_convert_fusion.59
  73.5 0.6 add_convert_fusion.60
  74.4 0.6 add_convert_fusion.61
  75.4 0.6 add_convert_fusion.62
  76.3 0.6 add_convert_fusion.63
  78.0 1.6 multiply_convert_fusion.11
  86.1 0.8 copy-done.9
  96.1 0.6 add_convert_fusion.56
  97.0 0.6 add_convert_fusion.57
  98.0 0.6 add_convert_fusion.58
  99.0 0.6 add_convert_fusion.59
  99.9 0.6 add_convert_fusion.60
  100.9 0.6 add_convert_fusion.61
  101.8 0.6 add_convert_fusion.62
  102.8 0.6 add_convert_fusion.63
  104.5 1.6 multiply_convert_fusion.11
  112.6 0.8 copy-done.9
  113.4 2.7 %scatter_custom_fusion = bf16[768,1152]{1,0:T(8,128)(2,1)S(1)} fusion(s32[256]{0:T(256)} %bitcast.610, bf16[256,1152]{1,0:T(8,128)(2,1)} %bitcast.614, bf16[]{:T(256)} %constant.112.clone.1), kind=kCustom, calls=%fused_computation.342 | custom fusion | bytes 1769984 | tf_op jit(solution)/shard_map/scatter | solution.py:116
  116.2 1.1 fusion.351
  117.3 1.7 fusion.350
  119.1 0.6 constant_dynamic-update-slice_fusion.32
  119.7 0.6 constant_dynamic-update-slice_fusion.31
  120.3 0.6 constant_dynamic-update-slice_fusion.30
  121.0 0.6 constant_dynamic-update-slice_fusion.29
  121.6 0.6 constant_dynamic-update-slice_fusion.28
  122.2 0.6 constant_dynamic-update-slice_fusion.27
  139.2 3.8 %all-to-all-start.1 = ((bf16[32,24,1,1152]{3,1,2,0:T(8,128)(2,1)}), bf16[32,24,1,1152]{3,1,2,0:T(8,128)(2,1)S(1)}, u32[]{:S(2)}, u32[]{:S(2)}) async-start(bf16[32,24,1,1152]{3,1,2,0:T(8,128)(2,1)} %constant_dynamic-update-slice_fusion.1), calls=%async_computation.1 | async-start | bytes 3538944 | tf_op jit(solution)/shard_map/all_to_all | solution.py:120
  143.9 40.9 %all-to-all-done.1 = bf16[32,24,1,1152]{3,1,2,0:T(8,128)(2,1)S(1)} async-done(((bf16[32,24,1,1152]{3,1,2,0:T(8,128)(2,1)}), bf16[32,24,1,1152]{3,1,2,0:T(8,128)(2,1)S(1)}, u32[]{:S(2)}, u32[]{:S(2)}) %all-to-all-start.1) | async-done | bytes 1769504 | tf_op jit(solution)/shard_map/all_to_all | solution.py:120
  184.8 0.7 fusion.331
  185.8 0.7 gather_fusion.1
  186.5 1.5 collective-permute-start
  188.5 3.3 %collective-permute-start.1 = (bf16[1,16,1152]{2,1,0:T(8,128)(2,1)S(1)}, bf16[1,16,1152]{2,1,0:T(8,128)(2,1)S(1)}, u32[]{:S(2)}, u32[]{:S(2)}) collective-permute-start(bf16[1,16,1152]{2,1,0:T(8,128)(2,1)S(1)} %get-tuple-element.647), channel_id=1, source_target_pairs={{4,0},{8,4},{12,8},{16,12},{20,16},{24,20},{28,24},{0,28},{5,1},{9... | collective-permute-start | bytes 110600 | tf_op jit(solution)/shard_map/ppermute | solution.py:23
  191.8 1.4 collective-permute-done
  193.7 3.9 %scatter_fusion = bf16[768,1152]{1,0:T(8,128)(2,1)} fusion(bf16[768,1152]{1,0:T(8,128)(2,1)} %bitcast.592, s32[64]{0:T(128)S(1)} %fusion.347, bf16[64,1152]{1,0:T(8,128)(2,1)S(1)} %bitcast.606), kind=kCustom, calls=%fused_computation.3 | custom fusion | bytes 442624 | tf_op jit(solution)/shard_map/scatter | solution.py:139
  (235 shorter events, 56.9 us)
Async XLA Ops:
  8.0 7.6 %copy-start.5 = (bf16[3,16,32]{2,1,0:T(8,128)(2,1)S(1)}, bf16[3,16,32]{2,1,0:T(8,128)(2,1)}, u32[]{:S(2)}) copy-start(bf16[3,16,32]{2,1,0:T(8,128)(2,1)} %param.23) | copy-start | bytes 9220
  8.0 7.6 %copy-start.4 = (bf16[3,32,96]{2,1,0:T(8,128)(2,1)S(1)}, bf16[3,32,96]{2,1,0:T(8,128)(2,1)}, u32[]{:S(2)}) copy-start(bf16[3,32,96]{2,1,0:T(8,128)(2,1)} %param.21) | copy-start | bytes 55300
  8.0 7.7 %copy-start.2 = (bf16[8,3,32,32]{3,2,1,0:T(8,128)(2,1)S(1)}, bf16[8,3,32,32]{3,2,1,0:T(8,128)(2,1)}, u32[]{:S(2)}) copy-start(bf16[8,3,32,32]{3,2,1,0:T(8,128)(2,1)} %param.18) | copy-start | bytes 147460
  8.0 7.8 %copy-start.3 = (bf16[8,3,32,32]{3,2,1,0:T(8,128)(2,1)S(1)}, bf16[8,3,32,32]{3,2,1,0:T(8,128)(2,1)}, u32[]{:S(2)}) copy-start(bf16[8,3,32,32]{3,2,1,0:T(8,128)(2,1)} %param.22) | copy-start | bytes 147460
  8.0 8.0 %copy-start.1 = (bf16[8,3,64,64]{3,2,1,0:T(8,128)(2,1)S(1)}, bf16[8,3,64,64]{3,2,1,0:T(8,128)(2,1)}, u32[]{:S(2)}) copy-start(bf16[8,3,64,64]{3,2,1,0:T(8,128)(2,1)} %param.20) | copy-start | bytes 589828
  8.0 49.3 %all-to-all-start = ((bf16[24,32,1152]{2,0,1:T(8,128)(2,1)}), bf16[24,32,1152]{2,0,1:T(8,128)(2,1)}, u32[]{:S(2)}, u32[]{:S(2)}) async-start(bf16[24,32,1152]{2,0,1:T(8,128)(2,1)} %copy.1202), calls=%async_computation | async-start | bytes 3538944 | tf_op jit(solution)/shard_map/all_to_all | solution.py:104
  37.7 21.3 %copy-start.7 = (s32[256,1]{0,1:T(1,128)}, s32[256,1]{0,1:T(1,128)S(1)}, u32[]{:S(2)}) copy-start(s32[256,1]{0,1:T(1,128)S(1)} %compare_select_fusion) | copy-start | bytes 3076
  59.0 1.3 copy-start.10
  59.0 1.3 copy-start.11
  85.0 1.1 copy-start.8
  86.1 0.8 copy-start.9
  111.5 1.1 copy-start.8
  112.6 0.8 copy-start.9
  139.2 4.5 %copy-start.6 = (s32[1,4,16]{2,1,0:T(4,128)S(1)}, s32[1,4,16]{2,1,0:T(4,128)}, u32[]{:S(2)}) copy-start(s32[1,4,16]{2,1,0:T(4,128)} %param.16) | copy-start | bytes 772
  139.2 45.6 %all-to-all-start.1 = ((bf16[32,24,1,1152]{3,1,2,0:T(8,128)(2,1)}), bf16[32,24,1,1152]{3,1,2,0:T(8,128)(2,1)S(1)}, u32[]{:S(2)}, u32[]{:S(2)}) async-start(bf16[32,24,1,1152]{3,1,2,0:T(8,128)(2,1)} %constant_dynamic-update-slice_fusion.1), calls=%async_computation.1 | async-start | bytes 3538944 | tf_op jit(solution)/shard_map/all_to_all | solution.py:120
  185.7 7.9 %copy-start = (bf16[24,32,1152]{2,1,0:T(8,128)(2,1)}, bf16[24,32,1152]{2,1,0:T(8,128)(2,1)S(1)}, u32[]{:S(2)}) copy-start(bf16[24,32,1152]{2,1,0:T(8,128)(2,1)S(1)} %copy.1211) | copy-start | bytes 5308420
  186.5 6.7 %collective-permute-start = (bf16[1,16,1152]{2,1,0:T(8,128)(2,1)S(1)}, bf16[1,16,1152]{2,1,0:T(8,128)(2,1)S(1)}, u32[]{:S(2)}, u32[]{:S(2)}) collective-permute-start(bf16[1,16,1152]{2,1,0:T(8,128)(2,1)S(1)} %get-tuple-element.644), channel_id=1, source_target_pairs={{0,4},{4,8},{8,12},{12,16},{16,20},{20,24},{24,28},{28,0},{1,5},{5... | collective-permute-start | bytes 110600 | tf_op jit(solution)/shard_map/ppermute | solution.py:21
  188.0 5.3 %collective-permute-start.3 = (bf16[1,16,1152]{2,1,0:T(8,128)(2,1)S(1)}, bf16[1,16,1152]{2,1,0:T(8,128)(2,1)S(1)}, u32[]{:S(2)}, u32[]{:S(2)}) collective-permute-start(bf16[1,16,1152]{2,1,0:T(8,128)(2,1)S(1)} %get-tuple-element.645), channel_id=1, source_target_pairs={{1,0},{2,1},{3,2},{0,3},{5,4},{6,5},{7,6},{4,7},{9,8},{10,9},{11,1... | collective-permute-start | bytes 110600 | tf_op jit(solution)/shard_map/ppermute | solution.py:23
  188.5 4.8 %collective-permute-start.2 = (bf16[1,16,1152]{2,1,0:T(8,128)(2,1)S(1)}, bf16[1,16,1152]{2,1,0:T(8,128)(2,1)S(1)}, u32[]{:S(2)}, u32[]{:S(2)}) collective-permute-start(bf16[1,16,1152]{2,1,0:T(8,128)(2,1)S(1)} %get-tuple-element.646), channel_id=1, source_target_pairs={{0,1},{1,2},{2,3},{3,0},{4,5},{5,6},{6,7},{7,4},{8,9},{9,10},{10,1... | collective-permute-start | bytes 110600 | tf_op jit(solution)/shard_map/ppermute | solution.py:21
  188.5 5.1 %collective-permute-start.1 = (bf16[1,16,1152]{2,1,0:T(8,128)(2,1)S(1)}, bf16[1,16,1152]{2,1,0:T(8,128)(2,1)S(1)}, u32[]{:S(2)}, u32[]{:S(2)}) collective-permute-start(bf16[1,16,1152]{2,1,0:T(8,128)(2,1)S(1)} %get-tuple-element.647), channel_id=1, source_target_pairs={{4,0},{8,4},{12,8},{16,12},{20,16},{24,20},{28,24},{0,28},{5,1},{9... | collective-permute-start | bytes 110600 | tf_op jit(solution)/shard_map/ppermute | solution.py:23
